TPU v7x, 256 devices: a whole 4x4x8 slice. The times are simulated.
256 devices in a mesh: cfg: 32 (over y, x, core), tm: 8 (over z).
Axes of the slice: x: 4, y: 4, z: 8, core: 2. Of those that a mesh axis runs over, the one named last changes fastest.
Arguments:
- targets: float32 [8192, 1024], P('cfg', 'tm'), may hold values from -6 to 6
- features: float32 [8192, 64], P('cfg'), may hold values from -6 to 6
- inv_scales: float32 [64], replicated, may hold values from 0.05 to 0.3
- noise: float32 [8192], P('cfg'), may hold values from 0.1 to 1
- time_kernel: float32 [1024, 1024], P('tm'), may hold values from -1 to 1, as said below
- block_mask: int32 [8192, 8], P('cfg', 'tm'), may hold values from 0 to 1, as said below
Outputs:
- solution_field: float32 [8192, 1024], P('cfg', 'tm')
- residual: float32 [8192, 1024], P('cfg', 'tm')
Inputs may be any that keep to these rules, and one draw needn't show every extreme that they name: `block_mask`: each configuration observes one contiguous run of blocks that starts at a block of 0 to 2 and has at least one block; some runs start late and some reach the last block. `time_kernel`: symmetric positive definite, with unit diagonal.
All inputs are finite; a program needn't handle non-finite values.
Results may differ from a plain program's by a relative error of at most 0.00026.
Values sent between devices are 32-bit elements; how exact they have to be, the bound alone decides.
A program may use at most 64 MiB of HBM per device.

v0:
```python
import jax
import jax.numpy as jnp
from jax import lax
from jax.sharding import PartitionSpec as P

BLOCK = 128
ITERS = 2


def matern(left, right):
    cross = jnp.dot(
        left, right.T, precision=lax.Precision.HIGHEST, preferred_element_type=jnp.float32
    )
    dist2 = (
        jnp.sum(left * left, axis=1)[:, None]
        + jnp.sum(right * right, axis=1)[None, :]
        - 2.0 * cross
    )
    scaled_dist = jnp.sqrt(3.0) * jnp.sqrt(jnp.maximum(dist2, 0.0))
    return (1.0 + scaled_dist) * jnp.exp(-scaled_dist)


def body(targets, features, inv_scales, noise, time_kernel, block_mask):
    mask = jnp.repeat(block_mask.astype(jnp.float32), BLOCK, axis=1)
    scaled = features * inv_scales[None, :]
    every = lax.all_gather(scaled, "cfg", axis=0, tiled=True)
    tile = matern(scaled, every)
    residual = mask * targets
    direction = residual
    solution_field = jnp.zeros_like(residual)
    norm_now = lax.psum(jnp.sum(residual * residual), ("cfg", "tm"))
    for step in range(ITERS):
        operate_mixed = jnp.dot(
            tile,
            lax.all_gather(mask * direction, "cfg", axis=0, tiled=True),
            precision=lax.Precision.HIGHEST,
            preferred_element_type=jnp.float32,
        )
        image = (
            mask
            * lax.psum_scatter(
                jnp.dot(
                    time_kernel.T,
                    operate_mixed.T,
                    precision=lax.Precision.HIGHEST,
                    preferred_element_type=jnp.float32,
                ),
                "tm",
                scatter_dimension=0,
                tiled=True,
            ).T
            + noise[:, None] * direction
        )
        curv = lax.psum(jnp.sum(direction * image), ("cfg", "tm"))
        alpha = norm_now / curv
        solution_field = solution_field + alpha * direction
        residual = residual - alpha * image
        norm_next = lax.psum(jnp.sum(residual * residual), ("cfg", "tm"))
        direction = residual + norm_next / norm_now * direction
        norm_now = norm_next
    return (solution_field, residual)


def solution(mesh):
    return jax.shard_map(
        body,
        mesh=mesh,
        in_specs=(P("cfg", "tm"), P("cfg", None), P(), P("cfg"), P("tm", None), P("cfg", "tm")),
        out_specs=(P("cfg", "tm"), P("cfg", "tm")),
        check_vma=False,
    )
```

profile of v0, /device:TPU:1, one launch (start us, length us, event | category | flops | bytes accessed | tf_op | source)
XLA Modules:
  0.0 509.3 jit_solution(8296447586257143950)
XLA Ops:
  7.2 0.0 copy-start
  7.2 0.0 all-gather.4.cloned.1.call-start
  7.2 1.6 multiply_reduce_fusion.5
  8.8 0.0 all-gather.4.cloned.1.call-update
  8.8 0.0 all-gather.6.cloned.1.call-start
  8.9 0.7 convert_element_type.5
  9.6 1.7 multiply_multiply_fusion
  11.2 0.0 all-gather.6.cloned.1.call-update
  11.3 0.0 reduce-scatter.3.cloned.1.call-start
  11.3 53.5 %all-gather.4.cloned.1.call-done = f32[8192,64]{0,1:T(8,128)} async-done(((f32[256,64]{0,1:T(8,128)}), f32[8192,64]{0,1:T(8,128)}) %all-gather.4.cloned.1.call-update) | async-done | bytes 2097168 | tf_op jit(solution)/shard_map/all_gather | solution.py:26
  64.8 1.8 multiply_reduce_fusion
  66.6 14.5 %exponential_multiply_fusion = f32[256,8192]{1,0:T(8,128)} fusion(f32[256,64]{0,1:T(8,128)} %get-tuple-element.7, f32[8192,64]{0,1:T(8,128)} %all-gather.4.cloned.1.call-done, f32[8192]{0:T(1024)S(1)} %multiply_reduce_fusion, f32[256]{0:T(256)S(1)} %get-tuple-element.6), kind=kOutput, calls=%fused_computation.5 | convolution fusion | flops 1627389952 | bytes 10585088 | tf_op jit(solution)/shard_map/dot_general | solution.py:11
  81.0 0.0 copy-start.1
  81.0 0.0 copy-start.3
  81.0 37.4 %all-gather.6.cloned.1.call-done = f32[8192,128]{1,0:T(8,128)} async-done(((f32[256,128]{1,0:T(8,128)}), f32[8192,128]{1,0:T(8,128)}) %all-gather.6.cloned.1.call-update) | async-done | bytes 4194320 | tf_op jit(solution)/shard_map/all_gather | solution.py:35
  118.5 9.8 %fusion.4 = f32[256,128]{1,0:T(8,128)S(1)} fusion(f32[256,8192]{1,0:T(8,128)} %exponential_multiply_fusion, f32[8192,128]{1,0:T(8,128)} %all-gather.6.cloned.1.call-done), kind=kOutput, calls=%fused_computation.23 | convolution fusion | flops 3221225472 | bytes 12713984 | tf_op jit(solution)/shard_map/dot_general | solution.py:33
  128.3 0.0 copy-done
  128.3 2.0 convolution_bitcast_fusion.1
  130.3 0.0 reduce-scatter.3.cloned.1.call-update
  130.4 0.0 all-gather.8.cloned.1.call-start
  130.4 33.7 %reduce-scatter.3.cloned.1.call-done = f32[128,256]{0,1:T(8,128)} async-done(((f32[1024,256]{0,1:T(8,128)}), f32[128,256]{0,1:T(8,128)}) %reduce-scatter.3.cloned.1.call-update) | async-done | bytes 131088 | tf_op jit(solution)/shard_map/reduce_scatter | solution.py:41
  164.1 0.0 copy-done.1
  164.1 0.0 copy-done.3
  164.1 0.0 copy-start.2
  164.1 1.8 multiply_reduce_fusion.3
  165.8 79.3 %all-reduce = (f32[]{:T(128)}, f32[]{:T(128)}) all-reduce(f32[]{:T(128)} %get-tuple-element.3, f32[]{:T(128)} %get-tuple-element.2), channel_id=1, replica_groups=mesh['cfg'=32,'tm'=8] {'cfg','tm'}, use_global_device_ids=true, to_apply=%region_1.0 | all-reduce | flops 2 | bytes 16 | tf_op jit(solution)/shard_map/psum | solution.py:31
  246.5 1.7 multiply_reduce_fusion.2
  248.2 73.5 %psum.30 = f32[]{:T(128)} all-reduce(f32[]{:T(128)} %multiply_reduce_fusion.2), channel_id=1, replica_groups=mesh['cfg'=32,'tm'=8] {'cfg','tm'}, use_global_device_ids=true, to_apply=%region_8.0 | all-reduce | flops 1 | bytes 8 | tf_op jit(solution)/shard_map/psum | solution.py:58
  323.0 1.7 broadcast_multiply_fusion
  324.8 0.0 all-gather.8.cloned.1.call-update
  324.8 0.0 reduce-scatter.5.cloned.1.call-start
  324.9 48.3 %all-gather.8.cloned.1.call-done = f32[8192,128]{1,0:T(8,128)} async-done(((f32[256,128]{1,0:T(8,128)}), f32[8192,128]{1,0:T(8,128)}) %all-gather.8.cloned.1.call-update) | async-done | bytes 4194320 | tf_op jit(solution)/shard_map/all_gather | solution.py:35
  373.2 9.8 %fusion.5 = f32[256,128]{1,0:T(8,128)S(1)} fusion(f32[256,8192]{1,0:T(8,128)} %exponential_multiply_fusion, f32[8192,128]{1,0:T(8,128)} %all-gather.8.cloned.1.call-done), kind=kOutput, calls=%fused_computation.24 | convolution fusion | flops 3221225472 | bytes 12713984 | tf_op jit(solution)/shard_map/dot_general | solution.py:33
  383.0 2.0 convolution_bitcast_fusion
  384.9 0.0 reduce-scatter.5.cloned.1.call-update
  385.0 33.1 %reduce-scatter.5.cloned.1.call-done = f32[128,256]{0,1:T(8,128)} async-done(((f32[1024,256]{0,1:T(8,128)}), f32[128,256]{0,1:T(8,128)}) %reduce-scatter.5.cloned.1.call-update) | async-done | bytes 131088 | tf_op jit(solution)/shard_map/reduce_scatter | solution.py:41
  418.1 0.0 copy-done.2
  418.1 1.7 multiply_reduce_fusion.1
  419.7 79.9 %psum.31 = f32[]{:T(128)} all-reduce(f32[]{:T(128)} %multiply_reduce_fusion.1), channel_id=1, replica_groups=mesh['cfg'=32,'tm'=8] {'cfg','tm'}, use_global_device_ids=true, to_apply=%region_11.0 | all-reduce | flops 1 | bytes 8 | tf_op jit(solution)/shard_map/psum | solution.py:54
  501.0 1.8 multiply_subtract_fusion
Async XLA Ops:
  7.2 121.1 %copy-start = (f32[128,1024]{1,0:T(8,128)S(1)}, f32[128,1024]{1,0:T(8,128)}, u32[]{:S(2)}) copy-start(f32[128,1024]{1,0:T(8,128)} %param.10) | copy-start | bytes 1572868
  7.2 57.6 %all-gather.4.cloned.1.call-start = ((), (), s32[]{:S(2)}) async-start(), calls=%async_computation.2 | async-start | bytes 2162688 | tf_op jit(solution)/shard_map/all_gather | solution.py:26
  8.8 109.6 %all-gather.6.cloned.1.call-start = ((), (), s32[]{:S(2)}) async-start(), calls=%async_computation.3 | async-start | bytes 4325376 | tf_op jit(solution)/shard_map/all_gather | solution.py:35
  11.3 152.8 %reduce-scatter.3.cloned.1.call-start = ((), (), s32[]{:S(2)}) async-start(), calls=%async_computation.4 | async-start | bytes 1179648 | tf_op jit(solution)/shard_map/reduce_scatter | solution.py:41
  81.0 83.0 %copy-start.1 = (f32[256,128]{1,0:T(8,128)S(1)}, f32[256,128]{1,0:T(8,128)}, u32[]{:S(2)}) copy-start(f32[256,128]{1,0:T(8,128)} %param.6) | copy-start | bytes 393220
  81.0 83.0 %copy-start.3 = (f32[256]{0:T(256)S(1)}, f32[256]{0:T(256)}, u32[]{:S(2)}) copy-start(f32[256]{0:T(256)} %param.9) | copy-start | bytes 3076
  130.4 242.8 %all-gather.8.cloned.1.call-start = ((), (), s32[]{:S(2)}) async-start(), calls=%async_computation.5 | async-start | bytes 4325376 | tf_op jit(solution)/shard_map/all_gather | solution.py:35
  164.1 254.0 %copy-start.2 = (f32[128,256]{0,1:T(8,128)S(1)}, f32[128,256]{0,1:T(8,128)}, u32[]{:S(2)}) copy-start(f32[128,256]{0,1:T(8,128)} %reduce-scatter.3.cloned.1.call-done) | copy-start | bytes 393220
  324.8 93.2 %reduce-scatter.5.cloned.1.call-start = ((), (), s32[]{:S(2)}) async-start(), calls=%async_computation.6 | async-start | bytes 1179648 | tf_op jit(solution)/shard_map/reduce_scatter | solution.py:41
Sparse Core Ops, SparseCore 0:
  11.0 53.7 all-gather.3
  67.9 50.5 all-gather.5
  130.5 33.5 reduce-scatter.2
  324.9 48.1 all-gather.7
  385.1 32.9 reduce-scatter.4
where the time goes:
time: 510 us; the launch traced here: 509 us
  blocking collectives  233 us (46%)
  waiting for transfers between devices  206 us (40%)
  matrix products  38.1 us (7%)
  between operations  17.8 us (3%)
  other arithmetic  14.4 us (3%)
    all_gather x2, waiting for transfers between devices, body(): lax.all_gather(mask * direction, 'cfg', axis=0, tiled=True)  85.7 us
    psum x1, blocking collectives, body(): curv = lax.psum(jnp.sum(direction * image), ('cfg', 'tm'))  79.9 us
    psum x1, blocking collectives, body(): norm_now = lax.psum(jnp.sum(residual * residual), ('cfg', 'tm'))  79.3 us
    psum x1, blocking collectives, body(): norm_next = lax.psum(jnp.sum(residual * residual), ('cfg', 'tm'))  73.5 us
    reduce_scatter x2, waiting for transfers between devices, body(): lax.psum_scatter(jnp.dot(time_kernel.T, operate_mixed.T, precision=lax.Pr...  66.7 us
    all_gather x1, waiting for transfers between devices, body(): every = lax.all_gather(scaled, 'cfg', axis=0, tiled=True)  53.5 us
    dot_general x2, matrix products, body(): jnp.dot(tile, lax.all_gather(mask * direction, 'cfg', axis=0, tiled=True)...  19.6 us
    dot_general x1, matrix products, matern(): jnp.dot(left, right.T, precision=lax.Precision.HIGHEST, preferred_element...  14.5 us
  transfers between devices with their start and end apart: 5, of which 5 were waited for; matrix products, arithmetic and copies ran while one was open for 4% of the time, Pallas kernels for 0%

commit v1 on v0

--- a/solution.py
+++ b/solution.py
@@ -23,7 +23,9 @@
 def body(targets, features, inv_scales, noise, time_kernel, block_mask):
     mask = jnp.repeat(block_mask.astype(jnp.float32), BLOCK, axis=1)
     scaled = features * inv_scales[None, :]
-    every = lax.all_gather(scaled, "cfg", axis=0, tiled=True)
+    every = jnp.concatenate(
+        lax.all_to_all(jnp.stack([scaled] * lax.axis_size("cfg")), "cfg", 0, 0), axis=0
+    )
     tile = matern(scaled, every)
     residual = mask * targets
     direction = residual

time: 510 us -> 468 us (0.918)
  waiting for transfers between devices: 206 us -> 128 us
  blocking collectives: 233 us -> 271 us
    all_gather x1 -> x0, waiting for transfers between devices: 53.5 us -> none  [body(): every = lax.all_gather(scaled, 'cfg', axis=0, tiled=True)]
    all_to_all x0 -> x1, blocking collectives: none -> 38.8 us  [body(): lax.all_to_all(jnp.stack([scaled] * lax.axis_size('cfg')), 'cfg', 0, 0)]
    all_gather x2, waiting for transfers between devices: 85.7 us -> 61.1 us  [body(): lax.all_gather(mask * direction, 'cfg', axis=0, tiled=True)]
  transfers between devices with their start and end apart: 5 -> 4, of which waited for: 5 -> 4; matrix products, arithmetic and copies ran while one was open for 4% -> 3% of each run, Pallas kernels for 0% -> 0%
where the time goes in v1:
time: 468 us; the launch traced here: 467 us
  blocking collectives  271 us (58%)
  waiting for transfers between devices  128 us (27%)
  matrix products  36.8 us (8%)
  between operations  17.8 us (4%)
  other arithmetic  12.2 us (3%)
    psum x1, blocking collectives, body(): curv = lax.psum(jnp.sum(direction * image), ('cfg', 'tm'))  79.7 us
    psum x1, blocking collectives, body(): norm_now = lax.psum(jnp.sum(residual * residual), ('cfg', 'tm'))  79.5 us
    psum x1, blocking collectives, body(): norm_next = lax.psum(jnp.sum(residual * residual), ('cfg', 'tm'))  73.2 us
    reduce_scatter x2, waiting for transfers between devices, body(): lax.psum_scatter(jnp.dot(time_kernel.T, operate_mixed.T, precision=lax.Pr...  67 us
    all_gather x2, waiting for transfers between devices, body(): lax.all_gather(mask * direction, 'cfg', axis=0, tiled=True)  61.1 us
    all_to_all x1, blocking collectives, body(): lax.all_to_all(jnp.stack([scaled] * lax.axis_size('cfg')), 'cfg', 0, 0)  38.8 us
    dot_general x2, matrix products, body(): jnp.dot(tile, lax.all_gather(mask * direction, 'cfg', axis=0, tiled=True)...  19.6 us
    dot_general x1, matrix products, matern(): jnp.dot(left, right.T, precision=lax.Precision.HIGHEST, preferred_element...  13.2 us
  transfers between devices with their start and end apart: 4, of which 4 were waited for; matrix products, arithmetic and copies ran while one was open for 3% of the time, Pallas kernels for 0%

profile of v1, /device:TPU:1, one launch (start us, length us, event | category | flops | bytes accessed | tf_op | source)
XLA Modules:
  0.0 466.8 jit_solution(6898170031612358138)
XLA Ops:
  7.2 0.0 copy-start
  7.2 0.0 all-gather.3.cloned.1.call-start
  7.2 0.7 convert_element_type.5
  8.0 1.7 multiply_multiply_fusion
  9.6 0.0 all-gather.3.cloned.1.call-update
  9.6 0.0 reduce-scatter.3.cloned.1.call-start
  9.7 0.9 multiply_reduce_fusion.5
  10.6 0.2 stack.2
  10.9 38.8 %all_to_all.5 = f32[32,256,64]{1,2,0:T(8,128)S(1)} all-to-all(f32[32,256,64]{1,2,0:T(8,128)S(1)} %stack.2), channel_id=1, replica_groups=mesh['cfg'=32,'tm'=8] {'cfg'}, dimensions={0} | all-to-all | bytes 4194304 | tf_op jit(solution)/shard_map/all_to_all | solution.py:27
  49.6 0.2 copy.10
  49.8 0.2 multiply_reduce_fusion
  50.1 13.2 %exponential_multiply_fusion = f32[256,8192]{1,0:T(8,128)} fusion(f32[256,64]{0,1:T(8,128)S(1)} %get-tuple-element.7, f32[8192,64]{0,1:T(8,128)S(1)} %bitcast.42, f32[8192]{0:T(1024)S(1)} %bitcast.50, f32[256]{0:T(256)S(1)} %get-tuple-element.6), kind=kOutput, calls=%fused_computation.5 | convolution fusion | flops 1627389952 | bytes 10585088 | tf_op jit(solution)/shard_map/dot_general | solution.py:11
  63.3 0.0 copy-start.1
  63.3 0.0 copy-start.3
  63.3 12.7 %all-gather.3.cloned.1.call-done = f32[8192,128]{1,0:T(8,128)} async-done(((f32[256,128]{1,0:T(8,128)}), f32[8192,128]{1,0:T(8,128)}) %all-gather.3.cloned.1.call-update) | async-done | bytes 4194320 | tf_op jit(solution)/shard_map/all_gather | solution.py:37
  76.0 9.8 %fusion.4 = f32[256,128]{1,0:T(8,128)S(1)} fusion(f32[256,8192]{1,0:T(8,128)} %exponential_multiply_fusion, f32[8192,128]{1,0:T(8,128)} %all-gather.3.cloned.1.call-done), kind=kOutput, calls=%fused_computation.23 | convolution fusion | flops 3221225472 | bytes 12713984 | tf_op jit(solution)/shard_map/dot_general | solution.py:35
  85.8 0.0 copy-done
  85.8 2.0 convolution_bitcast_fusion.1
  87.9 0.0 reduce-scatter.3.cloned.1.call-update
  87.9 0.0 all-gather.5.cloned.1.call-start
  87.9 33.8 %reduce-scatter.3.cloned.1.call-done = f32[128,256]{0,1:T(8,128)} async-done(((f32[1024,256]{0,1:T(8,128)}), f32[128,256]{0,1:T(8,128)}) %reduce-scatter.3.cloned.1.call-update) | async-done | bytes 131088 | tf_op jit(solution)/shard_map/reduce_scatter | solution.py:43
  121.7 0.0 copy-done.1
  121.7 0.0 copy-done.3
  121.7 0.0 copy-start.2
  121.7 1.8 multiply_reduce_fusion.3
  123.5 79.5 %all-reduce = (f32[]{:T(128)}, f32[]{:T(128)}) all-reduce(f32[]{:T(128)} %get-tuple-element.3, f32[]{:T(128)} %get-tuple-element.2), channel_id=1, replica_groups=mesh['cfg'=32,'tm'=8] {'cfg','tm'}, use_global_device_ids=true, to_apply=%region_1.0 | all-reduce | flops 2 | bytes 16 | tf_op jit(solution)/shard_map/psum | solution.py:33
  204.3 1.7 multiply_reduce_fusion.2
  206.0 73.2 %psum.30 = f32[]{:T(128)} all-reduce(f32[]{:T(128)} %multiply_reduce_fusion.2), channel_id=1, replica_groups=mesh['cfg'=32,'tm'=8] {'cfg','tm'}, use_global_device_ids=true, to_apply=%region_8.0 | all-reduce | flops 1 | bytes 8 | tf_op jit(solution)/shard_map/psum | solution.py:60
  280.5 1.7 broadcast_multiply_fusion
  282.3 0.0 all-gather.5.cloned.1.call-update
  282.3 0.0 reduce-scatter.5.cloned.1.call-start
  282.3 48.4 %all-gather.5.cloned.1.call-done = f32[8192,128]{1,0:T(8,128)} async-done(((f32[256,128]{1,0:T(8,128)}), f32[8192,128]{1,0:T(8,128)}) %all-gather.5.cloned.1.call-update) | async-done | bytes 4194320 | tf_op jit(solution)/shard_map/all_gather | solution.py:37
  330.7 9.8 %fusion.5 = f32[256,128]{1,0:T(8,128)S(1)} fusion(f32[256,8192]{1,0:T(8,128)} %exponential_multiply_fusion, f32[8192,128]{1,0:T(8,128)} %all-gather.5.cloned.1.call-done), kind=kOutput, calls=%fused_computation.24 | convolution fusion | flops 3221225472 | bytes 12713984 | tf_op jit(solution)/shard_map/dot_general | solution.py:35
  340.5 2.0 convolution_bitcast_fusion
  342.5 0.0 reduce-scatter.5.cloned.1.call-update
  342.5 33.3 %reduce-scatter.5.cloned.1.call-done = f32[128,256]{0,1:T(8,128)} async-done(((f32[1024,256]{0,1:T(8,128)}), f32[128,256]{0,1:T(8,128)}) %reduce-scatter.5.cloned.1.call-update) | async-done | bytes 131088 | tf_op jit(solution)/shard_map/reduce_scatter | solution.py:43
  375.8 0.0 copy-done.2
  375.8 1.7 multiply_reduce_fusion.1
  377.5 79.7 %psum.31 = f32[]{:T(128)} all-reduce(f32[]{:T(128)} %multiply_reduce_fusion.1), channel_id=1, replica_groups=mesh['cfg'=32,'tm'=8] {'cfg','tm'}, use_global_device_ids=true, to_apply=%region_11.0 | all-reduce | flops 1 | bytes 8 | tf_op jit(solution)/shard_map/psum | solution.py:56
  458.5 1.8 multiply_subtract_fusion
  (1 shorter events, 0.0 us)
Async XLA Ops:
  7.2 78.6 %copy-start = (f32[128,1024]{1,0:T(8,128)S(1)}, f32[128,1024]{1,0:T(8,128)}, u32[]{:S(2)}) copy-start(f32[128,1024]{1,0:T(8,128)} %param.10) | copy-start | bytes 1572868
  7.2 68.8 %all-gather.3.cloned.1.call-start = ((), (), s32[]{:S(2)}) async-start(), calls=%async_computation.3 | async-start | bytes 4325376 | tf_op jit(solution)/shard_map/all_gather | solution.py:37
  9.6 112.1 %reduce-scatter.3.cloned.1.call-start = ((), (), s32[]{:S(2)}) async-start(), calls=%async_computation.4 | async-start | bytes 1179648 | tf_op jit(solution)/shard_map/reduce_scatter | solution.py:43
  63.3 58.4 %copy-start.1 = (f32[256,128]{1,0:T(8,128)S(1)}, f32[256,128]{1,0:T(8,128)}, u32[]{:S(2)}) copy-start(f32[256,128]{1,0:T(8,128)} %param.6) | copy-start | bytes 393220
  63.3 58.4 %copy-start.3 = (f32[256]{0:T(256)S(1)}, f32[256]{0:T(256)}, u32[]{:S(2)}) copy-start(f32[256]{0:T(256)} %param.9) | copy-start | bytes 3076
  87.9 242.8 %all-gather.5.cloned.1.call-start = ((), (), s32[]{:S(2)}) async-start(), calls=%async_computation.5 | async-start | bytes 4325376 | tf_op jit(solution)/shard_map/all_gather | solution.py:37
  121.7 254.1 %copy-start.2 = (f32[128,256]{0,1:T(8,128)S(1)}, f32[128,256]{0,1:T(8,128)}, u32[]{:S(2)}) copy-start(f32[128,256]{0,1:T(8,128)} %reduce-scatter.3.cloned.1.call-done) | copy-start | bytes 393220
  282.3 93.5 %reduce-scatter.5.cloned.1.call-start = ((), (), s32[]{:S(2)}) async-start(), calls=%async_computation.6 | async-start | bytes 1179648 | tf_op jit(solution)/shard_map/reduce_scatter | solution.py:43
Sparse Core Ops, SparseCore 0:
  11.1 64.8 all-gather.2
  88.0 33.6 reduce-scatter.2
  282.4 48.2 all-gather.4
  342.6 33.1 reduce-scatter.4
